TPU v7x, 32 devices: a whole 2x2x4 slice. The times are simulated.
32 devices in a mesh: dp: 8 (over y, x, core), tensor: 4 (over z).
Axes of the slice: x: 2, y: 2, z: 4, core: 2. Of those that a mesh axis runs over, the one named last changes fastest.
Arguments:
- tokens: bfloat16 [16384, 2048], P(('dp', 'tensor')), may hold values from -6 to 6
- segments: int32 [8, 2048], P('dp'), may hold values from 0 to 7, never falling along the last dimension, each value on 1 to 1024 neighbouring positions
- ln_gain: float32 [2048], replicated, may hold values from 0.5 to 1.5
- ln_shift: float32 [2048], replicated, may hold values from -1.5 to 1.5
- qkv_weight: bfloat16 [2048, 3, 2048], P('dp', None, 'tensor'), may hold values from -0.125 to 0.125
- qkv_bias: float32 [3, 2048], P(None, 'tensor'), may hold values from -3 to 3
- out_weight: bfloat16 [2048, 2048], P('tensor', 'dp'), may hold values from -1 to 1
- out_bias: float32 [2048], replicated, may hold values from -3 to 3
- fc1_weight: bfloat16 [2048, 8192], P('dp', 'tensor'), may hold values from -0.125 to 0.125
- fc1_bias: float32 [8192], P('tensor'), may hold values from -3 to 3
- fc2_weight: bfloat16 [8192, 2048], P('tensor', 'dp'), may hold values from -0.0625 to 0.0625
- fc2_bias: float32 [2048], replicated, may hold values from -3 to 3
- cotangent: bfloat16 [16384, 2048], P(('dp', 'tensor')), may hold values from -6 to 6
Outputs:
- mixed: bfloat16 [16384, 2048], P(('dp', 'tensor'))
- input_grad: bfloat16 [16384, 2048], P(('dp', 'tensor'))
- qkv_weight_grad: float32 [2048, 3, 2048], P('dp', None, 'tensor')
- qkv_bias_grad: float32 [3, 2048], P(None, 'tensor')
- out_weight_grad: float32 [2048, 2048], P('tensor', 'dp')
- out_bias_grad: float32 [2048], replicated
- fc1_weight_grad: float32 [2048, 8192], P('dp', 'tensor')
- fc1_bias_grad: float32 [8192], P('tensor')
- fc2_weight_grad: float32 [8192, 2048], P('tensor', 'dp')
- fc2_bias_grad: float32 [2048], replicated
- gain_grad: float32 [2048], replicated
- shift_grad: float32 [2048], replicated
Inputs may be any that keep to these rules, and one draw needn't show every extreme that they name: `segments`: each row holds one data group's 2048 tokens; along a row the sequence numbers never fall, each sequence covers 1 to 1024 consecutive tokens, and some sequence covers exactly 1024.
All inputs are finite; a program needn't handle non-finite values.
Results may differ from a plain program's by a relative error of at most 0.013.
Values may be sent and summed in bfloat16 or wider, within the bound.
A program may use at most 320 MiB of HBM per device.

v0:
```python
import jax
import jax.numpy as jnp
from jax import lax
from jax.sharding import PartitionSpec as P

D = 2048
H = 32
HD = 64
ROT = 32
EPS = 1e-05
ROPE_BASE = 10000.0
NEGATIVE = -1e30


def contract_rows(left_op, right_op):
    return lax.dot_general(
        left_op, right_op, (((0,), (0,)), ((), ())), preferred_element_type=jnp.float32
    )


def contract_cols(left_op, right_op):
    return lax.dot_general(
        left_op, right_op, (((1,), (1,)), ((), ())), preferred_element_type=jnp.float32
    )


def gelu_tanh(values_in):
    return jax.nn.gelu(values_in, approximate=True)


def seq_positions(segment_row):
    row_count = segment_row.shape[0]
    row_index = jnp.arange(row_count, dtype=jnp.int32)
    seq_begins = jnp.concatenate([jnp.ones((1,), dtype=bool), segment_row[1:] != segment_row[:-1]])
    starts = lax.cummax(jnp.where(seq_begins, row_index, jnp.zeros_like(row_index)), axis=0)
    return row_index - starts


def rotary_tables(positions):
    half_rot = ROT // 2
    frequency = ROPE_BASE ** (-(jnp.arange(half_rot, dtype=jnp.float32) * 2.0) / ROT)
    angles = positions.astype(jnp.float32)[:, None] * frequency[None, :]
    return (jnp.cos(angles)[:, None, :], jnp.sin(angles)[:, None, :])


def rotate(heads_in, cosine_table, sine_table):
    half_rot = ROT // 2
    first_half = heads_in[..., :half_rot]
    second_half = heads_in[..., half_rot:ROT]
    return jnp.concatenate(
        [
            first_half * cosine_table - second_half * sine_table,
            second_half * cosine_table + first_half * sine_table,
            heads_in[..., ROT:],
        ],
        axis=-1,
    )


def allowed_block(segment_row, first_row, block_rows):
    key_count = segment_row.shape[0]
    query_index = first_row + jnp.arange(block_rows, dtype=jnp.int32)
    key_index = jnp.arange(key_count, dtype=jnp.int32)
    query_seg = lax.dynamic_slice_in_dim(segment_row, first_row, block_rows, 0)
    return (query_seg[:, None] == segment_row[None, :]) & (
        key_index[None, :] <= query_index[:, None]
    )


def attend(queries, key_rows, value_rows, segment_row, block_rows):
    group_rows = queries.shape[0]
    factor = HD ** (-0.5)

    def one_block(block_index):
        first_row = block_index * block_rows
        query_block = lax.dynamic_slice_in_dim(queries, first_row, block_rows, 0)
        raw_scores = (
            jnp.einsum("qhd,khd->hqk", query_block, key_rows, preferred_element_type=jnp.float32)
            * factor
        )
        allowed = allowed_block(segment_row, first_row, block_rows)
        scores = jnp.where(allowed[None], raw_scores, NEGATIVE)
        row_max = jnp.max(scores, axis=-1, keepdims=True)
        exponent = jnp.exp(scores - row_max)
        row_total = jnp.sum(exponent, axis=-1, keepdims=True)
        attn_probs = (exponent / row_total).astype(jnp.bfloat16)
        block_out = jnp.einsum(
            "hqk,khd->qhd", attn_probs, value_rows, preferred_element_type=jnp.float32
        )
        return (block_out, (row_max + jnp.log(row_total))[..., 0])

    block_out, log_norm = lax.map(one_block, jnp.arange(group_rows // block_rows, dtype=jnp.int32))
    return (block_out.reshape(group_rows, -1), log_norm)


def attend_back(queries, key_rows, value_rows, grad_mix, log_norm, segment_row, block_rows):
    group_rows = queries.shape[0]
    factor = HD ** (-0.5)

    def one_block(running, block_item):
        grad_keys, grad_values = running
        block_index, block_norm = block_item
        first_row = block_index * block_rows
        query_block = lax.dynamic_slice_in_dim(queries, first_row, block_rows, 0)
        grad_block = lax.dynamic_slice_in_dim(grad_mix, first_row, block_rows, 0)
        raw_scores = (
            jnp.einsum("qhd,khd->hqk", query_block, key_rows, preferred_element_type=jnp.float32)
            * factor
        )
        allowed = allowed_block(segment_row, first_row, block_rows)
        attn_probs = jnp.where(allowed[None], jnp.exp(raw_scores - block_norm[..., None]), 0.0)
        grad_values = grad_values + jnp.einsum(
            "hqk,qhd->khd",
            attn_probs.astype(jnp.bfloat16),
            grad_block,
            preferred_element_type=jnp.float32,
        )
        grad_probs = jnp.einsum(
            "qhd,khd->hqk", grad_block, value_rows, preferred_element_type=jnp.float32
        )
        inner = jnp.sum(attn_probs * grad_probs, axis=-1, keepdims=True)
        grad_scores = (attn_probs * (grad_probs - inner)).astype(jnp.bfloat16)
        grad_queries = (
            jnp.einsum("hqk,khd->qhd", grad_scores, key_rows, preferred_element_type=jnp.float32)
            * factor
        )
        grad_keys = (
            grad_keys
            + jnp.einsum(
                "hqk,qhd->khd", grad_scores, query_block, preferred_element_type=jnp.float32
            )
            * factor
        )
        return ((grad_keys, grad_values), grad_queries)

    zero_rows = jnp.zeros(queries.shape, jnp.float32)
    block_ids = jnp.arange(group_rows // block_rows, dtype=jnp.int32)
    (grad_keys, grad_values), grad_queries = lax.scan(
        one_block, (zero_rows, zero_rows), (block_ids, log_norm)
    )
    return (grad_queries.reshape(queries.shape), grad_keys, grad_values)


def local(
    tokens,
    segments,
    ln_gain,
    ln_shift,
    qkv_weight,
    qkv_bias,
    out_weight,
    out_bias,
    fc1_weight,
    fc1_bias,
    fc2_weight,
    fc2_bias,
    cotangent,
):
    heads_here = H // lax.axis_size("tensor")
    segment_row = segments[0]
    group_rows = segment_row.shape[0]
    block_rows = min(512, group_rows)
    x_local = tokens.astype(jnp.float32)
    row_mean = jnp.mean(x_local, axis=-1, keepdims=True)
    centred = x_local - row_mean
    inv_std = lax.rsqrt(jnp.mean(centred * centred, axis=-1, keepdims=True) + EPS)
    normalized = centred * inv_std
    normed = lax.all_gather(
        (normalized * ln_gain + ln_shift).astype(jnp.bfloat16), "tensor", axis=0, tiled=True
    )
    w_qkv, w_out, w_up, w_down = (
        lax.all_gather(qkv_weight, "dp", axis=0, tiled=True),
        lax.all_gather(out_weight, "dp", axis=1, tiled=True),
        lax.all_gather(fc1_weight, "dp", axis=0, tiled=True),
        lax.all_gather(fc2_weight, "dp", axis=1, tiled=True),
    )
    local_width = w_qkv.shape[2]
    flat_qkv = w_qkv.reshape(D, 3 * local_width)
    qkv_raw = jnp.dot(normed, flat_qkv, preferred_element_type=jnp.float32).reshape(
        group_rows, 3, local_width
    )
    qkv_raw = qkv_raw + qkv_bias[None]
    positions = seq_positions(segment_row)
    cosine_table, sine_table = rotary_tables(positions)
    queries = rotate(
        qkv_raw[:, 0].reshape(group_rows, heads_here, HD), cosine_table, sine_table
    ).astype(jnp.bfloat16)
    key_rows = rotate(
        qkv_raw[:, 1].reshape(group_rows, heads_here, HD), cosine_table, sine_table
    ).astype(jnp.bfloat16)
    value_rows = qkv_raw[:, 2].reshape(group_rows, heads_here, HD).astype(jnp.bfloat16)
    attended_f32, log_norm = attend(queries, key_rows, value_rows, segment_row, block_rows)
    attended = attended_f32.astype(jnp.bfloat16)
    hidden = jnp.dot(normed, w_up, preferred_element_type=jnp.float32) + fc1_bias
    activated = gelu_tanh(hidden).astype(jnp.bfloat16)
    block_sum = lax.psum_scatter(
        (
            jnp.dot(attended, w_out, preferred_element_type=jnp.float32)
            + jnp.dot(activated, w_down, preferred_element_type=jnp.float32)
        ).astype(jnp.bfloat16),
        "tensor",
        scatter_dimension=0,
        tiled=True,
    ).astype(jnp.float32)
    mixed = (x_local + block_sum + out_bias + fc2_bias).astype(jnp.bfloat16)
    w_qkv, w_out, w_up, w_down = (
        lax.all_gather(qkv_weight, "dp", axis=0, tiled=True),
        lax.all_gather(out_weight, "dp", axis=1, tiled=True),
        lax.all_gather(fc1_weight, "dp", axis=0, tiled=True),
        lax.all_gather(fc2_weight, "dp", axis=1, tiled=True),
    )
    flat_qkv = w_qkv.reshape(D, 3 * local_width)
    grad_full = lax.all_gather(cotangent, "tensor", axis=0, tiled=True)
    grad_act = contract_cols(grad_full, w_down)
    gelu_value, gelu_pull = jax.vjp(gelu_tanh, hidden)
    grad_hidden = gelu_pull(grad_act)[0].astype(jnp.bfloat16)
    grad_up = contract_rows(normed, grad_hidden)
    grad_up_bias = jnp.sum(grad_hidden.astype(jnp.float32), axis=0)
    grad_mix = (
        contract_cols(grad_full, w_out).astype(jnp.bfloat16).reshape(group_rows, heads_here, HD)
    )
    grad_queries, grad_keys, grad_values = attend_back(
        queries, key_rows, value_rows, grad_mix, log_norm, segment_row, block_rows
    )
    grad_qkv = jnp.stack(
        [
            rotate(grad_queries, cosine_table, -sine_table).reshape(group_rows, local_width),
            rotate(grad_keys, cosine_table, -sine_table).reshape(group_rows, local_width),
            grad_values.reshape(group_rows, local_width),
        ],
        axis=1,
    ).astype(jnp.bfloat16)
    grad_qkv_bias = jnp.sum(grad_qkv.astype(jnp.float32), axis=0)
    flat_grad = grad_qkv.reshape(group_rows, 3 * local_width)
    grad_qkv_w = contract_rows(normed, flat_grad).reshape(D, 3, local_width)
    grad_down = contract_rows(activated, grad_full)
    grad_out = contract_rows(attended, grad_full)
    summed_qkv, summed_out, summed_up, summed_down = (
        lax.psum_scatter(
            grad_qkv_w.astype(jnp.bfloat16), "dp", scatter_dimension=0, tiled=True
        ).astype(jnp.float32),
        lax.psum_scatter(
            grad_out.astype(jnp.bfloat16), "dp", scatter_dimension=1, tiled=True
        ).astype(jnp.float32),
        lax.psum_scatter(
            grad_up.astype(jnp.bfloat16), "dp", scatter_dimension=0, tiled=True
        ).astype(jnp.float32),
        lax.psum_scatter(
            grad_down.astype(jnp.bfloat16), "dp", scatter_dimension=1, tiled=True
        ).astype(jnp.float32),
    )
    grad_normed = lax.psum_scatter(
        (contract_cols(flat_grad, flat_qkv) + contract_cols(grad_hidden, w_up)).astype(
            jnp.bfloat16
        ),
        "tensor",
        scatter_dimension=0,
        tiled=True,
    ).astype(jnp.float32)
    grad_scaled = grad_normed * ln_gain
    input_grad = inv_std * (
        grad_scaled
        - jnp.mean(grad_scaled, axis=-1, keepdims=True)
        - normalized * jnp.mean(grad_scaled * normalized, axis=-1, keepdims=True)
    )
    input_grad = (input_grad + cotangent.astype(jnp.float32)).astype(jnp.bfloat16)
    gain_sum, shift_sum, output_sum = lax.psum(
        (
            jnp.sum(grad_normed * normalized, axis=0),
            jnp.sum(grad_normed, axis=0),
            jnp.sum(cotangent.astype(jnp.float32), axis=0),
        ),
        ("dp", "tensor"),
    )
    qkv_bias_sum, up_bias_sum = lax.psum((grad_qkv_bias, grad_up_bias), "dp")
    return (
        mixed,
        input_grad,
        summed_qkv,
        qkv_bias_sum,
        summed_out,
        output_sum,
        summed_up,
        up_bias_sum,
        summed_down,
        output_sum,
        gain_sum,
        shift_sum,
    )


def solution(mesh):
    in_specs = (
        P(("dp", "tensor"), None),
        P("dp", None),
        P(),
        P(),
        P("dp", None, "tensor"),
        P(None, "tensor"),
        P("tensor", "dp"),
        P(),
        P("dp", "tensor"),
        P("tensor"),
        P("tensor", "dp"),
        P(),
        P(("dp", "tensor"), None),
    )
    out_specs = (
        P(("dp", "tensor"), None),
        P(("dp", "tensor"), None),
        P("dp", None, "tensor"),
        P(None, "tensor"),
        P("tensor", "dp"),
        P(),
        P("dp", "tensor"),
        P("tensor"),
        P("tensor", "dp"),
        P(),
        P(),
        P(),
    )
    return jax.shard_map(local, mesh=mesh, in_specs=in_specs, out_specs=out_specs, check_vma=False)
```

profile of v0, /device:TPU:0, one launch (start us, length us, event | category | flops | bytes accessed | tf_op | source)
XLA Modules:
  0.0 1624.3 jit_solution(4911673076161956696)
XLA Ops:
  19.7 38.5 %all-gather.9.cloned.1.call-done = bf16[2048,3,512]{2,0,1:T(8,128)(2,1)} async-done(((bf16[256,3,512]{2,0,1:T(8,128)(2,1)}), bf16[2048,3,512]{2,0,1:T(8,128)(2,1)}) %all-gather.9.cloned.1.call-update) | async-done | bytes 6291472 | tf_op jit(solution)/shard_map/all_gather | solution.py:172
  67.0 143.0 %all-gather.7.cloned.1.call-done = bf16[2048,2048]{1,0:T(8,128)(2,1)} async-done(((bf16[512,2048]{1,0:T(8,128)(2,1)}), bf16[2048,2048]{1,0:T(8,128)(2,1)}) %all-gather.7.cloned.1.call-update) | async-done | bytes 8388624 | tf_op jit(solution)/shard_map/all_gather | solution.py:168
  233.0 196.4 %while.27 = (s32[]{:T(128)}, bf16[4,512,8,64]{1,3,2,0:T(8,128)(2,1)}, f32[4,8,512]{2,1,0:T(8,128)S(1)}, s32[4]{0:T(128)S(1)}, s32[2048]{0:T(1024)S(1)}, /*index=...) while((s32[]{:T(128)}, ...), condition=%wide.region_7.8_spmd, body=%wide.region_4.7_spmd.sunk | while | flops 2251289088 | bytes 110774976 | solution.py:92
  439.4 528.9 %while.28 = (s32[]{:T(128)}, f32[2048,8,64]{0,2,1:T(8,128)}, f32[2048,8,64]{0,2,1:T(8,128)}, f32[4,512,8,64]{1,0,3,2:T(4,128)}, s32[4]{0:T(128)S(1)}, /*index=5*...) while((s32[]{:T(128)}, f32[2048,8,64]{0,2,1:T(8,128)}, ...), condition=%wide.region_11.12_spmd.clone, body=%wide.region_9.11_spmd.clone.sunk | while | flops 5452853760 | bytes 284264672 | solution.py:138
  460.7 25.0 %multiply_reduce_fusion.2 = (f32[8,512]{1,0:T(8,128)S(1)}, f32[8,512,2048]{2,1,0:T(8,128)}) fusion(f32[8,512,2048]{2,1,0:T(8,128)} %fusion.132, f32[8,512]{1,0:T(8,128)S(1)} %dynamic-slice_bitcast_fusion.2, bf16[2048,8,64]{0,2,1:T(8,128)(2,1)S(1)} %get-tuple-element.464, bf16[2048,8,64]{0,2,1:T(8,128)(2,1)} %get-tuple-element.461, ...), kind=kOutput, calls=%fused_computation.18.clone.1 | convolution fusion | flops 1115680768 | bytes 70811648 | tf_op jit(solution)/shard_map/while/body/eval_jaxpr/qhd,khd->hqk/dot_general | solution.py:107
  485.6 28.1 %multiply_convert_fusion.5 = bf16[8,512,2048]{2,1,0:T(8,128)(2,1)} fusion(f32[8,512,2048]{2,1,0:T(8,128)} %get-tuple-element.383, f32[8,512,2048]{2,1,0:T(8,128)} %fusion.132, f32[8,512]{1,0:T(8,128)S(1)} %get-tuple-element.384), kind=kLoop, calls=%fused_computation.17.clone.1 | loop fusion | flops 25165824 | bytes 83902464 | tf_op jit(solution)/shard_map/while/body/eval_jaxpr/convert_element_type | solution.py:122
  523.5 21.0 %dynamic_update_slice.19 = f32[4,512,8,64]{1,0,3,2:T(4,128)} dynamic-update-slice(f32[4,512,8,64]{1,0,3,2:T(4,128)} %get-tuple-element.443, f32[1,512,8,64]{1,0,3,2:T(1,128)S(1)} %copy.52, s32[]{:T(128)} %get-tuple-element.440, s32[]{:T(128)} %constant.48.clone.1..sunk.1, s32[]{:T(128)} %constant.48.clone.1..sunk.1, s32[]{:T(128)} %constant.48.clone.1..sunk.1) | dynamic-update-slice | bytes 2097156 | tf_op jit(solution)/shard_map/while/body/jit(dynamic_update_index_in_dim)/dynamic_update_slice | solution.py:92
  591.3 24.9 %multiply_reduce_fusion.2 = (f32[8,512]{1,0:T(8,128)S(1)}, f32[8,512,2048]{2,1,0:T(8,128)}) fusion(f32[8,512,2048]{2,1,0:T(8,128)} %fusion.132, f32[8,512]{1,0:T(8,128)S(1)} %dynamic-slice_bitcast_fusion.2, bf16[2048,8,64]{0,2,1:T(8,128)(2,1)S(1)} %get-tuple-element.464, bf16[2048,8,64]{0,2,1:T(8,128)(2,1)} %get-tuple-element.461, ...), kind=kOutput, calls=%fused_computation.18.clone.1 | convolution fusion | flops 1115680768 | bytes 70811648 | tf_op jit(solution)/shard_map/while/body/eval_jaxpr/qhd,khd->hqk/dot_general | solution.py:107
  616.1 27.4 %multiply_convert_fusion.5 = bf16[8,512,2048]{2,1,0:T(8,128)(2,1)} fusion(f32[8,512,2048]{2,1,0:T(8,128)} %get-tuple-element.383, f32[8,512,2048]{2,1,0:T(8,128)} %fusion.132, f32[8,512]{1,0:T(8,128)S(1)} %get-tuple-element.384), kind=kLoop, calls=%fused_computation.17.clone.1 | loop fusion | flops 25165824 | bytes 83902464 | tf_op jit(solution)/shard_map/while/body/eval_jaxpr/convert_element_type | solution.py:122
  653.3 21.0 %dynamic_update_slice.19 = f32[4,512,8,64]{1,0,3,2:T(4,128)} dynamic-update-slice(f32[4,512,8,64]{1,0,3,2:T(4,128)} %get-tuple-element.443, f32[1,512,8,64]{1,0,3,2:T(1,128)S(1)} %copy.52, s32[]{:T(128)} %get-tuple-element.440, s32[]{:T(128)} %constant.48.clone.1..sunk.1, s32[]{:T(128)} %constant.48.clone.1..sunk.1, s32[]{:T(128)} %constant.48.clone.1..sunk.1) | dynamic-update-slice | bytes 2097156 | tf_op jit(solution)/shard_map/while/body/jit(dynamic_update_index_in_dim)/dynamic_update_slice | solution.py:92
  723.4 24.9 %multiply_reduce_fusion.2 = (f32[8,512]{1,0:T(8,128)S(1)}, f32[8,512,2048]{2,1,0:T(8,128)}) fusion(f32[8,512,2048]{2,1,0:T(8,128)} %fusion.132, f32[8,512]{1,0:T(8,128)S(1)} %dynamic-slice_bitcast_fusion.2, bf16[2048,8,64]{0,2,1:T(8,128)(2,1)S(1)} %get-tuple-element.464, bf16[2048,8,64]{0,2,1:T(8,128)(2,1)} %get-tuple-element.461, ...), kind=kOutput, calls=%fused_computation.18.clone.1 | convolution fusion | flops 1115680768 | bytes 70811648 | tf_op jit(solution)/shard_map/while/body/eval_jaxpr/qhd,khd->hqk/dot_general | solution.py:107
  748.3 27.4 %multiply_convert_fusion.5 = bf16[8,512,2048]{2,1,0:T(8,128)(2,1)} fusion(f32[8,512,2048]{2,1,0:T(8,128)} %get-tuple-element.383, f32[8,512,2048]{2,1,0:T(8,128)} %fusion.132, f32[8,512]{1,0:T(8,128)S(1)} %get-tuple-element.384), kind=kLoop, calls=%fused_computation.17.clone.1 | loop fusion | flops 25165824 | bytes 83902464 | tf_op jit(solution)/shard_map/while/body/eval_jaxpr/convert_element_type | solution.py:122
  855.6 24.9 %multiply_reduce_fusion.2 = (f32[8,512]{1,0:T(8,128)S(1)}, f32[8,512,2048]{2,1,0:T(8,128)}) fusion(f32[8,512,2048]{2,1,0:T(8,128)} %fusion.132, f32[8,512]{1,0:T(8,128)S(1)} %dynamic-slice_bitcast_fusion.2, bf16[2048,8,64]{0,2,1:T(8,128)(2,1)S(1)} %get-tuple-element.464, bf16[2048,8,64]{0,2,1:T(8,128)(2,1)} %get-tuple-element.461, ...), kind=kOutput, calls=%fused_computation.18.clone.1 | convolution fusion | flops 1115680768 | bytes 70811648 | tf_op jit(solution)/shard_map/while/body/eval_jaxpr/qhd,khd->hqk/dot_general | solution.py:107
  880.5 27.4 %multiply_convert_fusion.5 = bf16[8,512,2048]{2,1,0:T(8,128)(2,1)} fusion(f32[8,512,2048]{2,1,0:T(8,128)} %get-tuple-element.383, f32[8,512,2048]{2,1,0:T(8,128)} %fusion.132, f32[8,512]{1,0:T(8,128)S(1)} %get-tuple-element.384), kind=kLoop, calls=%fused_computation.17.clone.1 | loop fusion | flops 25165824 | bytes 83902464 | tf_op jit(solution)/shard_map/while/body/eval_jaxpr/convert_element_type | solution.py:122
  1038.6 24.4 %fusion.72 = f32[2048,2048]{1,0:T(8,128)} fusion(bf16[2048,2048]{1,0:T(8,128)(2,1)} %all-gather.7.cloned.1.call-done, bf16[2048,2048]{1,0:T(8,128)(2,1)} %all-gather.13.cloned.1.call-done), kind=kOutput, calls=%fused_computation.124 | convolution fusion | flops 17179869184 | bytes 33554432 | tf_op jit(solution)/shard_map/dot_general | solution.py:194
  1063.0 36.4 %convert_reduce_fusion = (f32[2048]{0:T(1024)}, bf16[2048,2048]{1,0:T(8,128)(2,1)}) fusion(f32[2048,2048]{1,0:T(8,128)} %fusion.72, f32[2048]{0:T(1024)S(1)} %copy-done.21, bf16[2048,2048]{1,0:T(8,128)(2,1)} %all-gather.17.cloned.1.call-done, bf16[2048,2048]{1,0:T(8,128)(2,1)} %all-gather.15.cloned.1.call-done), kind=kOutput, calls=%fused_computation.50 | convolution fusion | flops 17276336128 | bytes 41959424 | tf_op jit(solution)/shard_map/dot_general | solution.py:22
  1099.4 24.1 %convolution_convert_fusion.1 = bf16[2048,2048]{1,0:T(8,128)(2,1)} fusion(bf16[2048,2048]{1,0:T(8,128)(2,1)} %all-gather.7.cloned.1.call-done, bf16[2048,2048]{1,0:T(8,128)(2,1)} %get-tuple-element.220), kind=kOutput, calls=%fused_computation.60 | convolution fusion | flops 17184063488 | bytes 25165824 | tf_op jit(solution)/shard_map/dot_general | solution.py:16
  1123.5 27.1 %convolution_convert_fusion = bf16[2048,2048]{1,0:T(8,128)(2,1)} fusion(bf16[2048,2048]{1,0:T(8,128)(2,1)} %all-gather.17.cloned.1.call-done, f32[2048,2048]{1,0:T(8,128)} %fusion.72, f32[2048]{0:T(1024)S(1)} %copy-done.21), kind=kOutput, calls=%fused_computation.59 | convolution fusion | flops 17226006528 | bytes 33562624 | tf_op jit(solution)/shard_map/dot_general | solution.py:16
  1171.3 25.6 %fusion.33 = bf16[2048,2048]{1,0:T(8,128)(2,1)} fusion(f32[2048,2048,1]{1,0,2:T(8,128)} %fusion.73, bf16[2048,2048]{1,0:T(8,128)(2,1)} %get-tuple-element.220, bf16[2048,2048]{1,0:T(8,128)(2,1)} %all-gather.13.cloned.1.call-done), kind=kOutput, calls=%fused_computation.49 | convolution fusion | flops 17188257792 | bytes 41943040 | tf_op jit(solution)/shard_map/dot_general | solution.py:22
  1208.6 31.4 %add_convert_fusion = bf16[2048,2048]{1,0:T(8,128)(2,1)} fusion(f32[2048,2048]{1,0:T(8,128)} %fusion.71, bf16[2048,2048]{1,0:T(8,128)(2,1)} %all-gather.15.cloned.1.call-done, f32[2048,2048]{1,0:T(8,128)} %fusion.72, f32[2048]{0:T(1024)S(1)} %copy-done.21), kind=kOutput, calls=%fused_computation.51 | convolution fusion | flops 17230200832 | bytes 50339840 | tf_op jit(solution)/shard_map/dot_general | solution.py:199
  1240.7 24.5 %all-reduce.1 = (f32[3,512]{1,0:T(4,128)}, f32[2048]{0:T(1024)}) all-reduce(f32[3,512]{1,0:T(4,128)S(1)} %copy-done.15, f32[2048]{0:T(1024)S(1)} %copy-done.16), channel_id=1, replica_groups=mesh['dp'=8,'tensor'=4] {'dp'}, use_global_device_ids=true, to_apply=%region_17.18 | all-reduce | flops 3584 | bytes 28672 | tf_op jit(solution)/shard_map/psum | solution.py:275
  1277.0 144.1 %reduce-scatter.9.cloned.1.call-done = bf16[512,2048]{1,0:T(8,128)(2,1)} async-done(((bf16[2048,2048]{1,0:T(8,128)(2,1)}), bf16[512,2048]{1,0:T(8,128)(2,1)}) %reduce-scatter.9.cloned.1.call-update) | async-done | bytes 2097168 | tf_op jit(solution)/shard_map/reduce_scatter | solution.py:252
  1424.6 143.9 %reduce-scatter.7.cloned.1.call-done = bf16[512,2048]{1,0:T(8,128)(2,1)} async-done(((bf16[2048,2048]{1,0:T(8,128)(2,1)}), bf16[512,2048]{1,0:T(8,128)(2,1)}) %reduce-scatter.7.cloned.1.call-update) | async-done | bytes 2097168 | tf_op jit(solution)/shard_map/reduce_scatter | solution.py:196
  1575.1 41.5 %all-reduce = (f32[2048]{0:T(1024)S(1)}, f32[2048]{0:T(1024)}, f32[2048]{0:T(1024)}) all-reduce(f32[2048]{0:T(1024)S(1)} %get-tuple-element.237, f32[2048]{0:T(1024)S(1)} %get-tuple-element.168, f32[2048]{0:T(1024)S(1)} %get-tuple-element.171), channel_id=1, replica_groups=mesh['dp'=8,'tensor'=4] {'dp','tensor'}, use_global_device_ids=true, to_apply=%region_20.21 | all-reduce | flops 6144 | bytes 49152 | tf_op jit(solution)/shard_map/psum | solution.py:267
  (206 shorter events, 646.9 us)
Async XLA Ops:
  7.2 51.0 %all-gather.9.cloned.1.call-start = ((), (), s32[]{:S(2)}) async-start(), calls=%async_computation.7 | async-start | bytes 7077888 | tf_op jit(solution)/shard_map/all_gather | solution.py:172
  7.9 202.1 %all-gather.7.cloned.1.call-start = ((), (), s32[]{:S(2)}) async-start(), calls=%async_computation.6 | async-start | bytes 10485760 | tf_op jit(solution)/shard_map/all_gather | solution.py:168
  15.1 414.3 %all-gather.11.cloned.1.call-start = ((), (), s32[]{:S(2)}) async-start(), calls=%async_computation.8 | async-start | bytes 2359296 | tf_op jit(solution)/shard_map/all_gather | solution.py:173
  15.9 413.6 %all-gather.17.cloned.1.call-start = ((), (), s32[]{:S(2)}) async-start(), calls=%async_computation.12 | async-start | bytes 10485760 | tf_op jit(solution)/shard_map/all_gather | solution.py:213
  16.5 1022.1 %all-gather.13.cloned.1.call-start = ((), (), s32[]{:S(2)}) async-start(), calls=%async_computation.9 | async-start | bytes 9437184 | tf_op jit(solution)/shard_map/all_gather | solution.py:174
  17.0 1045.9 %all-gather.15.cloned.1.call-start = ((), (), s32[]{:S(2)}) async-start(), calls=%async_computation.10 | async-start | bytes 9437184 | tf_op jit(solution)/shard_map/all_gather | solution.py:175
  17.6 1247.6 %reduce-scatter.13.cloned.1.call-start = ((), (), s32[]{:S(2)}) async-start(), calls=%async_computation.15 | async-start | bytes 2359296 | tf_op jit(solution)/shard_map/reduce_scatter | solution.py:242
  19.7 211.1 %copy-start.7 = (f32[2048,16]{0,1:T(8,128)}, f32[2048,16]{0,1:T(8,128)S(1)}, u32[]{:S(2)}) copy-start(f32[2048,16]{0,1:T(8,128)S(1)} %get-tuple-element.246) | copy-start | bytes 393220
  19.7 190.3 %copy-start.20 = (f32[3,512]{1,0:T(4,128)S(1)}, f32[3,512]{1,0:T(4,128)}, u32[]{:S(2)}) copy-start(f32[3,512]{1,0:T(4,128)} %param.22) | copy-start | bytes 18436
  968.3 9.6 copy-start.8
  968.3 9.6 copy-start.9
  1001.1 9.0 copy-start.4
  1019.1 247.9 %reduce-scatter.11.cloned.1.call-start = ((), (), s32[]{:S(2)}) async-start(), calls=%async_computation.14 | async-start | bytes 7077888 | tf_op jit(solution)/shard_map/reduce_scatter | solution.py:239
  1038.5 24.5 %copy-start.21 = (f32[2048]{0:T(1024)S(1)}, f32[2048]{0:T(1024)}, u32[]{:S(2)}) copy-start(f32[2048]{0:T(1024)} %param.26) | copy-start | bytes 24580
  1038.5 231.0 %reduce-scatter.15.cloned.1.call-start = ((), (), s32[]{:S(2)}) async-start(), calls=%async_computation.16 | async-start | bytes 9437184 | tf_op jit(solution)/shard_map/reduce_scatter | solution.py:245
  1123.5 150.8 %reduce-scatter.17.cloned.1.call-start = ((), (), s32[]{:S(2)}) async-start(), calls=%async_computation.17 | async-start | bytes 9437184 | tf_op jit(solution)/shard_map/reduce_scatter | solution.py:248
  1150.6 270.4 %reduce-scatter.9.cloned.1.call-start = ((), (), s32[]{:S(2)}) async-start(), calls=%async_computation.13 | async-start | bytes 10485760 | tf_op jit(solution)/shard_map/reduce_scatter | solution.py:252
  1196.9 371.6 %reduce-scatter.7.cloned.1.call-start = ((), (), s32[]{:S(2)}) async-start(), calls=%async_computation.11 | async-start | bytes 10485760 | tf_op jit(solution)/shard_map/reduce_scatter | solution.py:196
  1240.0 181.1 %copy-start.1 = (bf16[512,2048]{1,0:T(8,128)(2,1)S(1)}, bf16[512,2048]{1,0:T(8,128)(2,1)}, u32[]{:S(2)}) copy-start(bf16[512,2048]{1,0:T(8,128)(2,1)} %param.17) | copy-start | bytes 6291460
  1240.0 181.0 %copy-start.10 = (f32[2048]{0:T(1024)S(1)}, f32[2048]{0:T(1024)}, u32[]{:S(2)}) copy-start(f32[2048]{0:T(1024)} %param.19) | copy-start | bytes 24580
  1240.1 181.0 %copy-start.12 = (f32[512]{0:T(512)S(1)}, f32[512]{0:T(512)}, u32[]{:S(2)}) copy-start(f32[512]{0:T(512)} %copy-done.11) | copy-start | bytes 6148
  1240.1 181.0 %copy-start.14 = (f32[512]{0:T(512)S(1)}, f32[512]{0:T(512)}, u32[]{:S(2)}) copy-start(f32[512]{0:T(512)} %copy-done.13) | copy-start | bytes 6148
  1267.0 301.5 %copy-start.18 = (f32[2048]{0:T(1024)S(1)}, f32[2048]{0:T(1024)}, u32[]{:S(2)}) copy-start(f32[2048]{0:T(1024)} %param.28) | copy-start | bytes 24580
  1267.0 301.5 %copy-start.19 = (f32[2048]{0:T(1024)S(1)}, f32[2048]{0:T(1024)}, u32[]{:S(2)}) copy-start(f32[2048]{0:T(1024)} %param.24) | copy-start | bytes 24580
  (10 other events, 41.1 us)
Sparse Core Ops, SparseCore 0:
  9.9 48.2 all-gather.8
  60.3 149.6 all-gather.6
  211.9 26.4 all-gather.10
  239.8 149.6 all-gather.16
  391.2 52.6 all-gather.12
  445.6 55.9 all-gather.14
  1019.2 39.2 reduce-scatter.12
  1062.3 61.7 reduce-scatter.10
  1127.5 71.2 reduce-scatter.14
  1202.5 71.6 reduce-scatter.16
  1276.6 144.4 reduce-scatter.8
  1423.3 145.1 reduce-scatter.6
where the time goes:
time: 1640 us; the launch traced here: 1620 us
  matrix products  701 us (43%)
  waiting for transfers between devices  475 us (29%)
  other arithmetic  221 us (13%)
  local copies, waits for them, and re-layouts  141 us (9%)
  blocking collectives  66 us (4%)
    dot_general x8, matrix products, one_block(): jnp.einsum('qhd,khd->hqk', query_block, key_rows, preferred_element_type=...  161 us
    reduce_scatter x1, waiting for transfers between devices, local(): lax.psum_scatter((contract_cols(flat_grad, flat_qkv) + contract_cols(grad...  144 us
    reduce_scatter x1, waiting for transfers between devices, local(): lax.psum_scatter((jnp.dot(attended, w_out, preferred_element_type=jnp.flo...  144 us
    all_gather x1, waiting for transfers between devices, local(): lax.all_gather((normalized * ln_gain + ln_shift).astype(jnp.bfloat16), 't...  143 us
    convert_element_type x4, other arithmetic, one_block(): grad_scores = (attn_probs * (grad_probs - inner)).astype(jnp.bfloat16)  110 us
    dot_general x4, matrix products, contract_cols(): lax.dot_general(left_op, right_op, (((1,), (1,)), ((), ())), preferred_el...  92.6 us
    dynamic_update_slice x8, local copies, waits for them, and re-layouts, attend(): lax.map(one_block, jnp.arange(group_rows // block_rows, dtype=jnp.int32))  88.3 us
    dot_general x4, matrix products, contract_rows(): lax.dot_general(left_op, right_op, (((0,), (0,)), ((), ())), preferred_el...  79.5 us
  transfers between devices with their start and end apart: 12, of which 5 were waited for; matrix products, arithmetic and copies ran while one was open for 65% of the time, Pallas kernels for 0%

commit v1 on v0

--- a/solution.py
+++ b/solution.py
@@ -10,6 +10,27 @@
 EPS = 1e-05
 ROPE_BASE = 10000.0
 NEGATIVE = -1e30
+
+
+def gather_around(x, axis, dim):
+    devices, index, rows = (lax.axis_size(axis), lax.axis_index(axis), x.shape[dim])
+    right = [(i, (i + 1) % devices) for i in range(devices)]
+    left = [(i, (i - 1) % devices) for i in range(devices)]
+    whole = jnp.zeros((*x.shape[:dim], devices * rows, *x.shape[dim + 1 :]), x.dtype)
+    whole = lax.dynamic_update_slice_in_dim(whole, x, index * rows, axis=dim)
+    from_left = from_right = x
+    middle = devices // 2
+    for turn in range(1, middle + 1):
+        from_left = lax.ppermute(from_left, axis, right)
+        whole = lax.dynamic_update_slice_in_dim(
+            whole, from_left, (index - turn) % devices * rows, axis=dim
+        )
+        if turn < devices - middle:
+            from_right = lax.ppermute(from_right, axis, left)
+            whole = lax.dynamic_update_slice_in_dim(
+                whole, from_right, (index + turn) % devices * rows, axis=dim
+            )
+    return whole
 
 
 def contract_rows(left_op, right_op):
@@ -165,9 +186,7 @@
     centred = x_local - row_mean
     inv_std = lax.rsqrt(jnp.mean(centred * centred, axis=-1, keepdims=True) + EPS)
     normalized = centred * inv_std
-    normed = lax.all_gather(
-        (normalized * ln_gain + ln_shift).astype(jnp.bfloat16), "tensor", axis=0, tiled=True
-    )
+    normed = gather_around((normalized * ln_gain + ln_shift).astype(jnp.bfloat16), "tensor", 0)
     w_qkv, w_out, w_up, w_down = (
         lax.all_gather(qkv_weight, "dp", axis=0, tiled=True),
         lax.all_gather(out_weight, "dp", axis=1, tiled=True),

time: 1640 us -> 1700 us (1.037)
  waiting for transfers between devices: 475 us -> 507 us
  local copies, waits for them, and re-layouts: 141 us -> 170 us
    ppermute x0 -> x3, waiting for transfers between devices: none -> 166 us  [the longest x2 114 us: gather_around(): from_left = lax.ppermute(from_left, axis, right)]
    all_gather x1 -> x0, waiting for transfers between devices: 143 us -> none  [local(): lax.all_gather((normalized * ln_gain + ln_shift).astype(jnp.bfloat16), 't...]
    reduce_scatter x1, waiting for transfers between devices: 1.95 us -> 50.8 us  [local(): lax.psum_scatter(grad_down.astype(jnp.bfloat16), 'dp', scatter_dimension=...]
    all_gather x1, waiting for transfers between devices: 38.5 us -> 0.01 us  [local(): lax.all_gather(qkv_weight, 'dp', axis=0, tiled=True)]
  transfers between devices with their start and end apart: 12 -> 14, of which waited for: 5 -> 6; matrix products, arithmetic and copies ran while one was open for 65% -> 64% of each run, Pallas kernels for 0% -> 0%
where the time goes in v1:
time: 1700 us
  matrix products  705 us (41%)
  waiting for transfers between devices  507 us (30%)
  other arithmetic  223 us (13%)
  local copies, waits for them, and re-layouts  170 us (10%)
  blocking collectives  64.5 us (4%)
    dot_general x8, matrix products, one_block(): jnp.einsum('qhd,khd->hqk', query_block, key_rows, preferred_element_type=...  160 us
    reduce_scatter x1, waiting for transfers between devices, local(): lax.psum_scatter((jnp.dot(attended, w_out, preferred_element_type=jnp.flo...  144 us
    reduce_scatter x1, waiting for transfers between devices, local(): lax.psum_scatter((contract_cols(flat_grad, flat_qkv) + contract_cols(grad...  144 us
    ppermute x2, waiting for transfers between devices, gather_around(): from_left = lax.ppermute(from_left, axis, right)  114 us
    convert_element_type x4, other arithmetic, one_block(): grad_scores = (attn_probs * (grad_probs - inner)).astype(jnp.bfloat16)  110 us
    dot_general x4, matrix products, contract_cols(): lax.dot_general(left_op, right_op, (((1,), (1,)), ((), ())), preferred_el...  91.1 us
    dynamic_update_slice x8, local copies, waits for them, and re-layouts, attend(): lax.map(one_block, jnp.arange(group_rows // block_rows, dtype=jnp.int32))  88.3 us
    dot_general x4, matrix products, contract_rows(): lax.dot_general(left_op, right_op, (((0,), (0,)), ((), ())), preferred_el...  78.7 us
  transfers between devices with their start and end apart: 14, of which 6 were waited for; matrix products, arithmetic and copies ran while one was open for 64% of the time, Pallas kernels for 0%

profile of v1, /device:TPU:0, one launch (start us, length us, event | category | flops | bytes accessed | tf_op | source)
XLA Modules:
  0.0 1696.3 jit_solution(8363502954862662522)
XLA Ops:
  20.0 46.8 %collective-permute-done = bf16[512,2048]{1,0:T(8,128)(2,1)} collective-permute-done((bf16[512,2048]{1,0:T(8,128)(2,1)}, bf16[512,2048]{1,0:T(8,128)(2,1)}, u32[]{:S(2)}, u32[]{:S(2)}) %collective-permute-start) | collective-permute-done | bytes 2097184 | tf_op jit(solution)/shard_map/ppermute | solution.py:24
  81.0 51.5 %collective-permute-done.1 = bf16[512,2048]{1,0:T(8,128)(2,1)} collective-permute-done((bf16[512,2048]{1,0:T(8,128)(2,1)}, bf16[512,2048]{1,0:T(8,128)(2,1)}, u32[]{:S(2)}, u32[]{:S(2)}) %collective-permute-start.1) | collective-permute-done | bytes 2097184 | tf_op jit(solution)/shard_map/ppermute | solution.py:29
  141.0 67.4 %collective-permute-done.2 = bf16[512,2048]{1,0:T(8,128)(2,1)} collective-permute-done((bf16[512,2048]{1,0:T(8,128)(2,1)}, bf16[512,2048]{1,0:T(8,128)(2,1)}, u32[]{:S(2)}, u32[]{:S(2)}) %collective-permute-start.2) | collective-permute-done | bytes 2097184 | tf_op jit(solution)/shard_map/ppermute | solution.py:24
  221.7 29.9 %broadcast_add_fusion = f32[2048,3,512]{0,2,1:T(8,128)S(1)} fusion(f32[3,512]{1,0:T(4,128)S(1)} %copy-done.21, bf16[2048,3,512]{0,2,1:T(8,128)(2,1)} %copy.37, bf16[2048,2048]{0,1:T(8,128)(2,1)} %constant_dynamic-update-slice_fusion), kind=kOutput, calls=%fused_computation.66 | convolution fusion | flops 12888047616 | bytes 27269120 | tf_op jit(solution)/shard_map/dot_general | solution.py:198
  256.9 194.8 %while.27 = (s32[]{:T(128)}, bf16[4,512,8,64]{1,3,2,0:T(8,128)(2,1)}, f32[4,8,512]{2,1,0:T(8,128)S(1)}, s32[4]{0:T(128)S(1)}, s32[2048]{0:T(1024)S(1)}, /*index=...) while((s32[]{:T(128)}, ...), condition=%wide.region_7.8_spmd, body=%wide.region_4.7_spmd.sunk | while | flops 2251289088 | bytes 110774480 | solution.py:113
  466.7 526.7 %while.28 = (s32[]{:T(128)}, f32[2048,8,64]{0,2,1:T(8,128)}, f32[2048,8,64]{0,2,1:T(8,128)}, f32[4,512,8,64]{1,0,3,2:T(4,128)}, s32[4]{0:T(128)S(1)}, /*index=5*...) while((s32[]{:T(128)}, f32[2048,8,64]{0,2,1:T(8,128)}, ...), condition=%wide.region_11.12_spmd.clone, body=%wide.region_9.11_spmd.clone.sunk | while | flops 5452853760 | bytes 284264704 | solution.py:159
  487.0 24.8 %multiply_reduce_fusion.2 = (f32[8,512]{1,0:T(8,128)S(1)}, f32[8,512,2048]{2,1,0:T(8,128)}) fusion(f32[8,512,2048]{2,1,0:T(8,128)} %fusion.132, f32[8,512]{1,0:T(8,128)S(1)} %dynamic-slice_bitcast_fusion.2, bf16[2048,8,64]{0,2,1:T(8,128)(2,1)S(1)} %get-tuple-element.464, bf16[2048,8,64]{0,2,1:T(8,128)(2,1)} %get-tuple-element.461, ...), kind=kOutput, calls=%fused_computation.18.clone.1 | convolution fusion | flops 1115680768 | bytes 70811648 | tf_op jit(solution)/shard_map/while/body/eval_jaxpr/qhd,khd->hqk/dot_general | solution.py:128
  511.8 27.4 %multiply_convert_fusion.5 = bf16[8,512,2048]{2,1,0:T(8,128)(2,1)} fusion(f32[8,512,2048]{2,1,0:T(8,128)} %get-tuple-element.383, f32[8,512,2048]{2,1,0:T(8,128)} %fusion.132, f32[8,512]{1,0:T(8,128)S(1)} %get-tuple-element.384), kind=kLoop, calls=%fused_computation.17.clone.1 | loop fusion | flops 25165824 | bytes 83902464 | tf_op jit(solution)/shard_map/while/body/eval_jaxpr/convert_element_type | solution.py:143
  616.8 24.8 %multiply_reduce_fusion.2 = (f32[8,512]{1,0:T(8,128)S(1)}, f32[8,512,2048]{2,1,0:T(8,128)}) fusion(f32[8,512,2048]{2,1,0:T(8,128)} %fusion.132, f32[8,512]{1,0:T(8,128)S(1)} %dynamic-slice_bitcast_fusion.2, bf16[2048,8,64]{0,2,1:T(8,128)(2,1)S(1)} %get-tuple-element.464, bf16[2048,8,64]{0,2,1:T(8,128)(2,1)} %get-tuple-element.461, ...), kind=kOutput, calls=%fused_computation.18.clone.1 | convolution fusion | flops 1115680768 | bytes 70811648 | tf_op jit(solution)/shard_map/while/body/eval_jaxpr/qhd,khd->hqk/dot_general | solution.py:128
  641.6 27.4 %multiply_convert_fusion.5 = bf16[8,512,2048]{2,1,0:T(8,128)(2,1)} fusion(f32[8,512,2048]{2,1,0:T(8,128)} %get-tuple-element.383, f32[8,512,2048]{2,1,0:T(8,128)} %fusion.132, f32[8,512]{1,0:T(8,128)S(1)} %get-tuple-element.384), kind=kLoop, calls=%fused_computation.17.clone.1 | loop fusion | flops 25165824 | bytes 83902464 | tf_op jit(solution)/shard_map/while/body/eval_jaxpr/convert_element_type | solution.py:143
  748.9 24.8 %multiply_reduce_fusion.2 = (f32[8,512]{1,0:T(8,128)S(1)}, f32[8,512,2048]{2,1,0:T(8,128)}) fusion(f32[8,512,2048]{2,1,0:T(8,128)} %fusion.132, f32[8,512]{1,0:T(8,128)S(1)} %dynamic-slice_bitcast_fusion.2, bf16[2048,8,64]{0,2,1:T(8,128)(2,1)S(1)} %get-tuple-element.464, bf16[2048,8,64]{0,2,1:T(8,128)(2,1)} %get-tuple-element.461, ...), kind=kOutput, calls=%fused_computation.18.clone.1 | convolution fusion | flops 1115680768 | bytes 70811648 | tf_op jit(solution)/shard_map/while/body/eval_jaxpr/qhd,khd->hqk/dot_general | solution.py:128
  773.7 27.4 %multiply_convert_fusion.5 = bf16[8,512,2048]{2,1,0:T(8,128)(2,1)} fusion(f32[8,512,2048]{2,1,0:T(8,128)} %get-tuple-element.383, f32[8,512,2048]{2,1,0:T(8,128)} %fusion.132, f32[8,512]{1,0:T(8,128)S(1)} %get-tuple-element.384), kind=kLoop, calls=%fused_computation.17.clone.1 | loop fusion | flops 25165824 | bytes 83902464 | tf_op jit(solution)/shard_map/while/body/eval_jaxpr/convert_element_type | solution.py:143
  881.0 24.8 %multiply_reduce_fusion.2 = (f32[8,512]{1,0:T(8,128)S(1)}, f32[8,512,2048]{2,1,0:T(8,128)}) fusion(f32[8,512,2048]{2,1,0:T(8,128)} %fusion.132, f32[8,512]{1,0:T(8,128)S(1)} %dynamic-slice_bitcast_fusion.2, bf16[2048,8,64]{0,2,1:T(8,128)(2,1)S(1)} %get-tuple-element.464, bf16[2048,8,64]{0,2,1:T(8,128)(2,1)} %get-tuple-element.461, ...), kind=kOutput, calls=%fused_computation.18.clone.1 | convolution fusion | flops 1115680768 | bytes 70811648 | tf_op jit(solution)/shard_map/while/body/eval_jaxpr/qhd,khd->hqk/dot_general | solution.py:128
  905.8 27.4 %multiply_convert_fusion.5 = bf16[8,512,2048]{2,1,0:T(8,128)(2,1)} fusion(f32[8,512,2048]{2,1,0:T(8,128)} %get-tuple-element.383, f32[8,512,2048]{2,1,0:T(8,128)} %fusion.132, f32[8,512]{1,0:T(8,128)S(1)} %get-tuple-element.384), kind=kLoop, calls=%fused_computation.17.clone.1 | loop fusion | flops 25165824 | bytes 83902464 | tf_op jit(solution)/shard_map/while/body/eval_jaxpr/convert_element_type | solution.py:143
  1066.7 24.7 %fusion.72 = f32[2048,2048]{1,0:T(8,128)} fusion(bf16[2048,2048]{0,1:T(8,128)(2,1)} %constant_dynamic-update-slice_fusion, bf16[2048,2048]{1,0:T(8,128)(2,1)} %all-gather.10.cloned.1.call-done), kind=kOutput, calls=%fused_computation.128 | convolution fusion | flops 17179869184 | bytes 33554432 | tf_op jit(solution)/shard_map/dot_general | solution.py:213
  1091.3 36.3 %convert_reduce_fusion = (f32[2048]{0:T(1024)}, bf16[2048,2048]{1,0:T(8,128)(2,1)}) fusion(f32[2048,2048]{1,0:T(8,128)} %fusion.72, f32[2048]{0:T(1024)S(1)} %copy-done.22, bf16[2048,2048]{1,0:T(8,128)(2,1)} %all-gather.14.cloned.1.call-done, bf16[2048,2048]{1,0:T(8,128)(2,1)} %all-gather.12.cloned.1.call-done), kind=kOutput, calls=%fused_computation.50 | convolution fusion | flops 17276336128 | bytes 41959424 | tf_op jit(solution)/shard_map/dot_general | solution.py:43
  1127.7 23.9 %convolution_convert_fusion.1 = bf16[2048,2048]{1,0:T(8,128)(2,1)} fusion(bf16[2048,2048]{0,1:T(8,128)(2,1)} %constant_dynamic-update-slice_fusion, bf16[2048,2048]{1,0:T(8,128)(2,1)} %get-tuple-element.220), kind=kOutput, calls=%fused_computation.60 | convolution fusion | flops 17184063488 | bytes 25165824 | tf_op jit(solution)/shard_map/dot_general | solution.py:37
  1151.6 27.1 %convolution_convert_fusion = bf16[2048,2048]{1,0:T(8,128)(2,1)} fusion(bf16[2048,2048]{1,0:T(8,128)(2,1)} %all-gather.14.cloned.1.call-done, f32[2048,2048]{1,0:T(8,128)} %fusion.72, f32[2048]{0:T(1024)S(1)} %copy-done.22), kind=kOutput, calls=%fused_computation.59 | convolution fusion | flops 17226006528 | bytes 33562624 | tf_op jit(solution)/shard_map/dot_general | solution.py:37
  1198.2 25.4 %fusion.33 = bf16[2048,2048]{1,0:T(8,128)(2,1)} fusion(f32[2048,2048,1]{1,0,2:T(8,128)} %fusion.73, bf16[2048,2048]{1,0:T(8,128)(2,1)} %get-tuple-element.220, bf16[2048,2048]{1,0:T(8,128)(2,1)} %all-gather.10.cloned.1.call-done), kind=kOutput, calls=%fused_computation.49 | convolution fusion | flops 17188257792 | bytes 41943040 | tf_op jit(solution)/shard_map/dot_general | solution.py:43
  1236.0 28.8 %add_convert_fusion = bf16[2048,2048]{1,0:T(8,128)(2,1)} fusion(f32[2048,2048]{1,0:T(8,128)} %fusion.71, bf16[2048,2048]{1,0:T(8,128)(2,1)} %all-gather.12.cloned.1.call-done, f32[2048,2048]{1,0:T(8,128)} %fusion.72, f32[2048]{0:T(1024)S(1)} %copy-done.22), kind=kOutput, calls=%fused_computation.51 | convolution fusion | flops 17230200832 | bytes 50339840 | tf_op jit(solution)/shard_map/dot_general | solution.py:218
  1295.7 50.8 %reduce-scatter.17.cloned.1.call-done = bf16[2048,256]{1,0:T(8,128)(2,1)} async-done(((bf16[2048,2048]{1,0:T(8,128)(2,1)}), bf16[2048,256]{1,0:T(8,128)(2,1)}) %reduce-scatter.17.cloned.1.call-update) | async-done | bytes 1048592 | tf_op jit(solution)/shard_map/reduce_scatter | solution.py:267
  1349.2 144.0 %reduce-scatter.9.cloned.1.call-done = bf16[512,2048]{1,0:T(8,128)(2,1)} async-done(((bf16[2048,2048]{1,0:T(8,128)(2,1)}), bf16[512,2048]{1,0:T(8,128)(2,1)}) %reduce-scatter.9.cloned.1.call-update) | async-done | bytes 2097168 | tf_op jit(solution)/shard_map/reduce_scatter | solution.py:271
  1496.7 144.1 %reduce-scatter.7.cloned.1.call-done = bf16[512,2048]{1,0:T(8,128)(2,1)} async-done(((bf16[2048,2048]{1,0:T(8,128)(2,1)}), bf16[512,2048]{1,0:T(8,128)(2,1)}) %reduce-scatter.7.cloned.1.call-update) | async-done | bytes 2097168 | tf_op jit(solution)/shard_map/reduce_scatter | solution.py:215
  1647.4 41.5 %all-reduce = (f32[2048]{0:T(1024)S(1)}, f32[2048]{0:T(1024)}, f32[2048]{0:T(1024)}) all-reduce(f32[2048]{0:T(1024)S(1)} %get-tuple-element.237, f32[2048]{0:T(1024)S(1)} %get-tuple-element.168, f32[2048]{0:T(1024)S(1)} %get-tuple-element.171), channel_id=1, replica_groups=mesh['dp'=8,'tensor'=4] {'dp','tensor'}, use_global_device_ids=true, to_apply=%region_20.21 | all-reduce | flops 6144 | bytes 49152 | tf_op jit(solution)/shard_map/psum | solution.py:286
  (220 shorter events, 724.8 us)
Async XLA Ops:
  7.2 205.6 %all-gather.6.cloned.1.call-start = ((), (), s32[]{:S(2)}) async-start(), calls=%async_computation.6 | async-start | bytes 7077888 | tf_op jit(solution)/shard_map/all_gather | solution.py:191
  7.9 448.9 %all-gather.8.cloned.1.call-start = ((), (), s32[]{:S(2)}) async-start(), calls=%async_computation.7 | async-start | bytes 2359296 | tf_op jit(solution)/shard_map/all_gather | solution.py:192
  8.7 448.2 %all-gather.14.cloned.1.call-start = ((), (), s32[]{:S(2)}) async-start(), calls=%async_computation.11 | async-start | bytes 10485760 | tf_op jit(solution)/shard_map/all_gather | solution.py:232
  9.4 1057.2 %all-gather.10.cloned.1.call-start = ((), (), s32[]{:S(2)}) async-start(), calls=%async_computation.8 | async-start | bytes 9437184 | tf_op jit(solution)/shard_map/all_gather | solution.py:193
  10.0 1081.3 %all-gather.12.cloned.1.call-start = ((), (), s32[]{:S(2)}) async-start(), calls=%async_computation.9 | async-start | bytes 9437184 | tf_op jit(solution)/shard_map/all_gather | solution.py:194
  12.0 58.2 %copy-start.5 = (s32[1,2048]{1,0:T(1,128)S(1)}, s32[1,2048]{1,0:T(1,128)}, u32[]{:S(2)}) copy-start(s32[1,2048]{1,0:T(1,128)} %param.18) | copy-start | bytes 24580
  12.0 63.3 %copy-start.11 = (f32[512]{0:T(512)}, f32[512]{0:T(512)S(1)}, u32[]{:S(2)}) copy-start(f32[512]{0:T(512)S(1)} %broadcast_multiply_fusion.2) | copy-start | bytes 6148
  12.8 58.0 %copy-start.13 = (f32[512]{0:T(512)}, f32[512]{0:T(512)S(1)}, u32[]{:S(2)}) copy-start(f32[512]{0:T(512)S(1)} %add_rsqrt_fusion) | copy-start | bytes 6148
  14.9 51.9 %collective-permute-start = (bf16[512,2048]{1,0:T(8,128)(2,1)}, bf16[512,2048]{1,0:T(8,128)(2,1)}, u32[]{:S(2)}, u32[]{:S(2)}) collective-permute-start(bf16[512,2048]{1,0:T(8,128)(2,1)} %fusion.57), channel_id=1, source_target_pairs={{0,1},{1,2},{2,3},{3,0},{4,5},{5,6},{6,7},{7,4},{8,9},{9,10},{10,1... | collective-permute-start | bytes 6291464 | tf_op jit(solution)/shard_map/ppermute | solution.py:24
  17.9 114.5 %collective-permute-start.1 = (bf16[512,2048]{1,0:T(8,128)(2,1)}, bf16[512,2048]{1,0:T(8,128)(2,1)}, u32[]{:S(2)}, u32[]{:S(2)}) collective-permute-start(bf16[512,2048]{1,0:T(8,128)(2,1)} %fusion.57), channel_id=1, source_target_pairs={{0,3},{1,0},{2,1},{3,2},{4,7},{5,4},{6,5},{7,6},{8,11},{9,8},{10,9... | collective-permute-start | bytes 6291464 | tf_op jit(solution)/shard_map/ppermute | solution.py:29
  66.8 141.6 %collective-permute-start.2 = (bf16[512,2048]{1,0:T(8,128)(2,1)}, bf16[512,2048]{1,0:T(8,128)(2,1)}, u32[]{:S(2)}, u32[]{:S(2)}) collective-permute-start(bf16[512,2048]{1,0:T(8,128)(2,1)} %collective-permute-done), channel_id=1, source_target_pairs={{0,1},{1,2},{2,3},{3,0},{4,5},{5,6},{6,7},{7,4},{8,9},{9,10},{10,1... | collective-permute-start | bytes 6291464 | tf_op jit(solution)/shard_map/ppermute | solution.py:24
  66.8 1221.7 %reduce-scatter.13.cloned.1.call-start = ((), (), s32[]{:S(2)}) async-start(), calls=%async_computation.14 | async-start | bytes 2359296 | tf_op jit(solution)/shard_map/reduce_scatter | solution.py:261
  78.0 176.7 %copy-start.6 = (f32[2048,16]{0,1:T(8,128)}, f32[2048,16]{0,1:T(8,128)S(1)}, u32[]{:S(2)}) copy-start(f32[2048,16]{0,1:T(8,128)S(1)} %get-tuple-element.246) | copy-start | bytes 393220
  1047.8 242.6 %reduce-scatter.11.cloned.1.call-start = ((), (), s32[]{:S(2)}) async-start(), calls=%async_computation.13 | async-start | bytes 7077888 | tf_op jit(solution)/shard_map/reduce_scatter | solution.py:258
  1066.6 226.3 %reduce-scatter.15.cloned.1.call-start = ((), (), s32[]{:S(2)}) async-start(), calls=%async_computation.15 | async-start | bytes 9437184 | tf_op jit(solution)/shard_map/reduce_scatter | solution.py:264
  1151.5 195.0 %reduce-scatter.17.cloned.1.call-start = ((), (), s32[]{:S(2)}) async-start(), calls=%async_computation.16 | async-start | bytes 9437184 | tf_op jit(solution)/shard_map/reduce_scatter | solution.py:267
  1178.7 314.5 %reduce-scatter.9.cloned.1.call-start = ((), (), s32[]{:S(2)}) async-start(), calls=%async_computation.12 | async-start | bytes 10485760 | tf_op jit(solution)/shard_map/reduce_scatter | solution.py:271
  1223.7 417.1 %reduce-scatter.7.cloned.1.call-start = ((), (), s32[]{:S(2)}) async-start(), calls=%async_computation.10 | async-start | bytes 10485760 | tf_op jit(solution)/shard_map/reduce_scatter | solution.py:215
  1264.7 228.5 %copy-start.1 = (bf16[512,2048]{1,0:T(8,128)(2,1)S(1)}, bf16[512,2048]{1,0:T(8,128)(2,1)}, u32[]{:S(2)}) copy-start(bf16[512,2048]{1,0:T(8,128)(2,1)} %param.17) | copy-start | bytes 6291460
  1264.8 228.5 %copy-start.10 = (f32[2048]{0:T(1024)S(1)}, f32[2048]{0:T(1024)}, u32[]{:S(2)}) copy-start(f32[2048]{0:T(1024)} %param.19) | copy-start | bytes 24580
  1264.8 228.4 %copy-start.12 = (f32[512]{0:T(512)S(1)}, f32[512]{0:T(512)}, u32[]{:S(2)}) copy-start(f32[512]{0:T(512)} %copy-done.11) | copy-start | bytes 6148
  1264.8 228.4 %copy-start.14 = (f32[512]{0:T(512)S(1)}, f32[512]{0:T(512)}, u32[]{:S(2)}) copy-start(f32[512]{0:T(512)} %copy-done.13) | copy-start | bytes 6148
  1290.3 350.5 %copy-start.19 = (f32[2048]{0:T(1024)S(1)}, f32[2048]{0:T(1024)}, u32[]{:S(2)}) copy-start(f32[2048]{0:T(1024)} %param.28) | copy-start | bytes 24580
  1290.3 350.5 %copy-start.20 = (f32[2048]{0:T(1024)S(1)}, f32[2048]{0:T(1024)}, u32[]{:S(2)}) copy-start(f32[2048]{0:T(1024)} %param.24) | copy-start | bytes 24580
  (13 other events, 89.7 us)
Sparse Core Ops, SparseCore 0:
  9.9 48.2 all-gather.5
  60.1 28.1 all-gather.7
  89.9 201.1 all-gather.13
  292.9 53.5 all-gather.9
  348.2 55.9 all-gather.11
  1047.9 82.5 reduce-scatter.12
  1134.3 61.7 reduce-scatter.10
  1199.6 71.2 reduce-scatter.14
  1274.7 71.7 reduce-scatter.16
  1348.7 144.4 reduce-scatter.8
  1495.6 145.1 reduce-scatter.6
